TPU v7x, 32 devices: a whole 2x2x4 slice. The times are simulated.
32 devices in a mesh: dp: 8 (over y, x, core), fsdp: 4 (over z).
Axes of the slice: x: 2, y: 2, z: 4, core: 2. Of those that a mesh axis runs over, the one named last changes fastest.
Arguments:
- patches: bfloat16 [2, 2048, 1152], P(None, ('dp', 'fsdp')), may hold values from -6 to 6
- cotangent: bfloat16 [2, 2048, 1152], P(None, ('dp', 'fsdp')), may hold values from -6 to 6
- conditioning: float32 [2, 8, 1152], replicated, may hold values from -6 to 6
- frame_of_slot: int32 [2, 2048], P(None, ('dp', 'fsdp')), may hold values from 0 to 127, as said below
- clip_of_slot: int32 [2, 2048], P(None, ('dp', 'fsdp')), may hold values from 0 to 7, as said below
- w_ada: bfloat16 [1152, 6912], P('dp', 'fsdp'), may hold values from -0.1875 to 0.1875
- b_ada: bfloat16 [6912], P('fsdp'), may hold values from -3 to 3
- w_qkv: bfloat16 [1152, 3456], P('dp', 'fsdp'), may hold values from -0.1875 to 0.1875
- b_qv: bfloat16 [2304], P('fsdp'), may hold values from -2 to 2
- w_proj: bfloat16 [1152, 1152], P('dp', 'fsdp'), may hold values from -1 to 1
- b_proj: bfloat16 [1152], P('fsdp'), may hold values from -2 to 2
- w_fc1: bfloat16 [1152, 4608], P('dp', 'fsdp'), may hold values from -0.1875 to 0.1875
- b_fc1: bfloat16 [4608], P('fsdp'), may hold values from -3 to 3
- w_fc2: bfloat16 [4608, 1152], P('dp', 'fsdp'), may hold values from -0.09375 to 0.09375
- b_fc2: bfloat16 [1152], P('fsdp'), may hold values from -2 to 2
Outputs:
- output: bfloat16 [2, 2048, 1152], P(None, ('dp', 'fsdp'))
- input_grad: bfloat16 [2, 2048, 1152], P(None, ('dp', 'fsdp'))
- cond_grad: float32 [2, 8, 1152], P(None, None, 'fsdp')
- grad_w_ada: float32 [1152, 6912], P('dp', 'fsdp')
- grad_b_ada: float32 [6912], P('fsdp')
- grad_w_qkv: float32 [1152, 3456], P('dp', 'fsdp')
- grad_b_qv: float32 [2304], P('fsdp')
- grad_w_proj: float32 [1152, 1152], P('dp', 'fsdp')
- grad_b_proj: float32 [1152], P('fsdp')
- grad_w_fc1: float32 [1152, 4608], P('dp', 'fsdp')
- grad_b_fc1: float32 [4608], P('fsdp')
- grad_w_fc2: float32 [4608, 1152], P('dp', 'fsdp')
- grad_b_fc2: float32 [1152], P('fsdp')
Inputs may be any that keep to these rules, and one draw needn't show every extreme that they name: `frame_of_slot`: in each micro-batch, each aligned block of 64 slots holds either one frame of 64 patches or four frames of 16 patches one after another; no frame number appears in two blocks. `clip_of_slot`: all slots of one frame name the same clip.
All inputs are finite; a program needn't handle non-finite values.
Results may differ from a plain program's by a relative error of at most 0.018.
Values may be sent and summed in bfloat16 or wider, within the bound.
A program may use at most 256 MiB of HBM per device.

v0:
```python
import math
import jax
import jax.numpy as jnp
from jax import lax
from jax.sharding import PartitionSpec as P

HEAD_DIM = 72
EPS = 1e-06
GELU_C = math.sqrt(2.0 / math.pi)
PRECISE = lax.Precision.HIGHEST
NEG_FILL = -1e30


def layer_norm(values):
    centre = values - jnp.mean(values, axis=-1, keepdims=True)
    return centre * lax.rsqrt(jnp.mean(centre * centre, axis=-1, keepdims=True) + EPS)


def gelu_tanh(hidden):
    return 0.5 * hidden * (1.0 + jnp.tanh(GELU_C * (hidden + 0.044715 * hidden * hidden * hidden)))


def modulate(values, shift_part, scale_part):
    return layer_norm(values) * (1.0 + scale_part) + shift_part


def matmul_plain(left, right):
    return jnp.dot(left, right, preferred_element_type=jnp.float32)


def matmul_right_t(left, right):
    return lax.dot_general(
        left, right, (((1,), (1,)), ((), ())), preferred_element_type=jnp.float32
    )


def matmul_left_t(left, right):
    return lax.dot_general(
        left, right, (((0,), (0,)), ((), ())), preferred_element_type=jnp.float32
    )


def precise_left_t(left, right):
    return lax.dot_general(
        left, right, (((0,), (0,)), ((), ())), precision=PRECISE, preferred_element_type=jnp.float32
    )


def precise_right_t(left, right):
    return lax.dot_general(
        left, right, (((1,), (1,)), ((), ())), precision=PRECISE, preferred_element_type=jnp.float32
    )


def gather_weights(w_qkv, w_proj, w_fc1, w_fc2, b_qv, b_proj, b_fc1, b_fc2):
    inner_parts = (
        lax.all_gather(w_qkv, "fsdp", axis=1, tiled=True),
        lax.all_gather(w_proj, "fsdp", axis=1, tiled=True),
        lax.all_gather(w_fc1, "fsdp", axis=1, tiled=True),
        lax.all_gather(w_fc2, "fsdp", axis=1, tiled=True),
        lax.all_gather(b_qv, "fsdp", axis=0, tiled=True),
        lax.all_gather(b_proj, "fsdp", axis=0, tiled=True),
        lax.all_gather(b_fc1, "fsdp", axis=0, tiled=True),
        lax.all_gather(b_fc2, "fsdp", axis=0, tiled=True),
    )
    whole_rows = (
        lax.all_gather(inner_parts[0], "dp", axis=0, tiled=True),
        lax.all_gather(inner_parts[1], "dp", axis=0, tiled=True),
        lax.all_gather(inner_parts[2], "dp", axis=0, tiled=True),
        lax.all_gather(inner_parts[3], "dp", axis=0, tiled=True),
    )
    return (
        whole_rows[0],
        whole_rows[1],
        whole_rows[2],
        whole_rows[3],
        inner_parts[4],
        inner_parts[5],
        inner_parts[6],
        inner_parts[7],
    )


def reduce_grads(full_w, full_b):
    inner_sums = (
        lax.psum_scatter(
            full_w[0].astype(jnp.bfloat16), "fsdp", scatter_dimension=1, tiled=True
        ).astype(jnp.float32),
        lax.psum_scatter(
            full_w[1].astype(jnp.bfloat16), "fsdp", scatter_dimension=1, tiled=True
        ).astype(jnp.float32),
        lax.psum_scatter(
            full_w[2].astype(jnp.bfloat16), "fsdp", scatter_dimension=1, tiled=True
        ).astype(jnp.float32),
        lax.psum_scatter(
            full_w[3].astype(jnp.bfloat16), "fsdp", scatter_dimension=1, tiled=True
        ).astype(jnp.float32),
        lax.psum_scatter(
            full_b[0].astype(jnp.bfloat16), "fsdp", scatter_dimension=0, tiled=True
        ).astype(jnp.float32),
        lax.psum_scatter(
            full_b[1].astype(jnp.bfloat16), "fsdp", scatter_dimension=0, tiled=True
        ).astype(jnp.float32),
        lax.psum_scatter(
            full_b[2].astype(jnp.bfloat16), "fsdp", scatter_dimension=0, tiled=True
        ).astype(jnp.float32),
        lax.psum_scatter(
            full_b[3].astype(jnp.bfloat16), "fsdp", scatter_dimension=0, tiled=True
        ).astype(jnp.float32),
    )
    outer_sums = (
        lax.psum_scatter(
            inner_sums[0].astype(jnp.bfloat16), "dp", scatter_dimension=0, tiled=True
        ).astype(jnp.float32),
        lax.psum_scatter(
            inner_sums[1].astype(jnp.bfloat16), "dp", scatter_dimension=0, tiled=True
        ).astype(jnp.float32),
        lax.psum_scatter(
            inner_sums[2].astype(jnp.bfloat16), "dp", scatter_dimension=0, tiled=True
        ).astype(jnp.float32),
        lax.psum_scatter(
            inner_sums[3].astype(jnp.bfloat16), "dp", scatter_dimension=0, tiled=True
        ).astype(jnp.float32),
    )
    small_sums = lax.psum((inner_sums[4], inner_sums[5], inner_sums[6], inner_sums[7]), "dp")
    return (tuple(outer_sums), tuple(small_sums))


def modulation_sharded(silu_low, w_ada, b_ada):
    row_width, col_width = w_ada.shape
    row_start = lax.axis_index("dp") * row_width
    col_start = lax.axis_index("fsdp") * col_width
    silu_part = lax.dynamic_slice_in_dim(silu_low, row_start, row_width, 1)
    partial_value = matmul_plain(silu_part, w_ada)
    bias_term = jnp.where(
        lax.axis_index("dp") == 0, b_ada.astype(jnp.float32), jnp.zeros((col_width,), jnp.float32)
    )
    partial_value = partial_value + bias_term[None, :]
    padded = jnp.zeros((silu_low.shape[0], col_width * lax.axis_size("fsdp")), jnp.float32)
    padded = lax.dynamic_update_slice_in_dim(padded, partial_value, col_start, 1)
    return lax.psum(padded, ("dp", "fsdp"))


def ada_grads_sharded(silu_low, cond_rows, d_modulation, w_ada):
    row_width, col_width = w_ada.shape
    row_start = lax.axis_index("dp") * row_width
    col_start = lax.axis_index("fsdp") * col_width
    d_total = lax.psum(d_modulation, ("dp", "fsdp"))
    d_cols = lax.dynamic_slice_in_dim(d_total, col_start, col_width, 1)
    silu_part = lax.dynamic_slice_in_dim(silu_low, row_start, row_width, 1).astype(jnp.float32)
    grad_weight = precise_left_t(silu_part, d_cols)
    grad_bias = jnp.sum(d_cols, axis=0)
    d_silu_part = precise_right_t(d_cols, w_ada.astype(jnp.float32))
    model_width = cond_rows.shape[1]
    padded = jnp.zeros((cond_rows.shape[0], model_width), jnp.float32)
    padded = lax.dynamic_update_slice_in_dim(padded, d_silu_part, row_start, 1)
    d_silu = lax.psum(padded, ("dp", "fsdp"))
    own_width = model_width // lax.axis_size("fsdp")
    own_start = lax.axis_index("fsdp") * own_width
    d_silu_own = lax.dynamic_slice_in_dim(d_silu, own_start, own_width, 1)
    cond_own = lax.dynamic_slice_in_dim(cond_rows, own_start, own_width, 1)
    silu_own, silu_own_back = jax.vjp(jax.nn.silu, cond_own)
    cond_grad = silu_own_back(d_silu_own)[0]
    return (grad_weight, grad_bias, cond_grad)


def head_scores(queries, key_rows, same_frame):
    scores = jnp.einsum(
        "qhd,khd->hqk", queries, key_rows, preferred_element_type=jnp.float32
    ) * HEAD_DIM ** (-0.5)
    return jnp.where(same_frame[None, :, :], scores, NEG_FILL)


def micro_forward(patch_rows, modulation, frame_ids, clip_ids, weights):
    w_qkv, w_proj, w_fc1, w_fc2, b_qv, b_proj, b_fc1, b_fc2 = weights
    row_count, model_width = patch_rows.shape
    head_count = model_width // HEAD_DIM
    clip_hot = (
        clip_ids[:, None] == jnp.arange(modulation.shape[0], dtype=jnp.int32)[None, :]
    ).astype(jnp.float32)
    token_mod = jnp.dot(clip_hot, modulation, precision=PRECISE)
    shift_one, scale_one, gate_one, shift_two, scale_two, gate_two = jnp.split(token_mod, 6, axis=1)
    inputs_float = patch_rows.astype(jnp.float32)
    attn_in, norm_one_back = jax.vjp(modulate, inputs_float, shift_one, scale_one)
    attn_low = attn_in.astype(jnp.bfloat16)
    qkv_bias = jnp.concatenate(
        [b_qv[:model_width], jnp.zeros((model_width,), jnp.bfloat16), b_qv[model_width:]]
    ).astype(jnp.float32)
    qkv_low = (matmul_plain(attn_low, w_qkv) + qkv_bias).astype(jnp.bfloat16)
    queries = qkv_low[:, :model_width].reshape(row_count, head_count, HEAD_DIM)
    key_rows = qkv_low[:, model_width : 2 * model_width].reshape(row_count, head_count, HEAD_DIM)
    value_rows = qkv_low[:, 2 * model_width :].reshape(row_count, head_count, HEAD_DIM)
    same_frame = frame_ids[:, None] == frame_ids[None, :]
    scores = head_scores(queries, key_rows, same_frame)
    row_max = jnp.max(scores, axis=-1, keepdims=True)
    exp_scores = jnp.exp(scores - row_max)
    exp_total = jnp.sum(exp_scores, axis=-1, keepdims=True)
    shares = exp_scores / exp_total
    log_total = row_max + jnp.log(exp_total)
    mixed_low = (
        jnp.einsum(
            "hqk,khd->qhd",
            shares.astype(jnp.bfloat16),
            value_rows,
            preferred_element_type=jnp.float32,
        )
        .reshape(row_count, model_width)
        .astype(jnp.bfloat16)
    )
    attn_out = matmul_plain(mixed_low, w_proj) + b_proj.astype(jnp.float32)
    after_attn = inputs_float + gate_one * attn_out
    mlp_in, norm_two_back = jax.vjp(modulate, after_attn, shift_two, scale_two)
    mlp_low = mlp_in.astype(jnp.bfloat16)
    hidden = matmul_plain(mlp_low, w_fc1) + b_fc1.astype(jnp.float32)
    act_value, gelu_back = jax.vjp(gelu_tanh, hidden)
    act_low = act_value.astype(jnp.bfloat16)
    branch = matmul_plain(act_low, w_fc2) + b_fc2.astype(jnp.float32)
    output = (after_attn + gate_two * branch).astype(jnp.bfloat16)
    saved = (
        clip_hot,
        gate_one,
        gate_two,
        norm_one_back,
        attn_low,
        queries,
        key_rows,
        value_rows,
        same_frame,
        log_total,
        mixed_low,
        attn_out,
        norm_two_back,
        mlp_low,
        gelu_back,
        act_low,
        branch,
    )
    return (output, saved)


def micro_backward(saved, cot_rows, weights):
    w_qkv, w_proj, w_fc1, w_fc2 = (weights[0], weights[1], weights[2], weights[3])
    (
        clip_hot,
        gate_one,
        gate_two,
        norm_one_back,
        attn_low,
        queries,
        key_rows,
        value_rows,
        same_frame,
        log_total,
        mixed_low,
        attn_out,
        norm_two_back,
        mlp_low,
        gelu_back,
        act_low,
        branch,
    ) = saved
    row_count = cot_rows.shape[0]
    model_width = cot_rows.shape[1]
    head_count = model_width // HEAD_DIM
    cot_float = cot_rows.astype(jnp.float32)
    d_branch = (gate_two * cot_float).astype(jnp.bfloat16)
    grad_gate_two = cot_float * branch
    grad_w_fc2 = matmul_left_t(act_low, d_branch)
    grad_b_fc2 = jnp.sum(d_branch.astype(jnp.float32), axis=0)
    d_act = matmul_right_t(d_branch, w_fc2)
    d_hidden = gelu_back(d_act)[0].astype(jnp.bfloat16)
    grad_w_fc1 = matmul_left_t(mlp_low, d_hidden)
    grad_b_fc1 = jnp.sum(d_hidden.astype(jnp.float32), axis=0)
    d_mlp = matmul_right_t(d_hidden, w_fc1)
    d_after, d_shift_two, d_scale_two = norm_two_back(d_mlp)
    d_after = cot_float + d_after
    grad_gate_one = d_after * attn_out
    d_attn = (gate_one * d_after).astype(jnp.bfloat16)
    grad_w_proj = matmul_left_t(mixed_low, d_attn)
    grad_b_proj = jnp.sum(d_attn.astype(jnp.float32), axis=0)
    d_mix = (
        matmul_right_t(d_attn, w_proj).astype(jnp.bfloat16).reshape(row_count, head_count, HEAD_DIM)
    )
    shares_again = jnp.exp(head_scores(queries, key_rows, same_frame) - log_total)
    d_shares = jnp.einsum("qhd,khd->hqk", d_mix, value_rows, preferred_element_type=jnp.float32)
    row_delta = jnp.sum(shares_again * d_shares, axis=-1, keepdims=True)
    d_scores = (shares_again * (d_shares - row_delta)).astype(jnp.bfloat16)
    d_queries = jnp.einsum(
        "hqk,khd->qhd", d_scores, key_rows, preferred_element_type=jnp.float32
    ) * HEAD_DIM ** (-0.5)
    d_keys = jnp.einsum(
        "hqk,qhd->khd", d_scores, queries, preferred_element_type=jnp.float32
    ) * HEAD_DIM ** (-0.5)
    d_values = jnp.einsum(
        "hqk,qhd->khd", shares_again.astype(jnp.bfloat16), d_mix, preferred_element_type=jnp.float32
    )
    d_qkv = jnp.concatenate(
        [
            d_queries.reshape(row_count, model_width),
            d_keys.reshape(row_count, model_width),
            d_values.reshape(row_count, model_width),
        ],
        axis=1,
    ).astype(jnp.bfloat16)
    grad_w_qkv = matmul_left_t(attn_low, d_qkv)
    column_sums = jnp.sum(d_qkv.astype(jnp.float32), axis=0)
    grad_b_qv = jnp.concatenate([column_sums[:model_width], column_sums[2 * model_width :]])
    d_attn_in = matmul_right_t(d_qkv, w_qkv)
    d_inputs, d_shift_one, d_scale_one = norm_one_back(d_attn_in)
    input_grad = (d_after + d_inputs).astype(jnp.bfloat16)
    d_token_mod = jnp.concatenate(
        [d_shift_one, d_scale_one, grad_gate_one, d_shift_two, d_scale_two, grad_gate_two], axis=1
    )
    d_modulation = lax.dot_general(
        clip_hot,
        d_token_mod,
        (((0,), (0,)), ((), ())),
        precision=PRECISE,
        preferred_element_type=jnp.float32,
    )
    grads_w = (grad_w_qkv, grad_w_proj, grad_w_fc1, grad_w_fc2)
    grads_b = (grad_b_qv, grad_b_proj, grad_b_fc1, grad_b_fc2)
    return (input_grad, d_modulation, grads_w, grads_b)


def add_terms(first_terms, second_terms):
    if first_terms is None:
        return tuple(second_terms)
    return tuple(
        (first_item + second_item for first_item, second_item in zip(first_terms, second_terms))
    )


def per_device(
    patches,
    cotangent,
    conditioning,
    frame_of_slot,
    clip_of_slot,
    w_ada,
    b_ada,
    w_qkv,
    b_qv,
    w_proj,
    b_proj,
    w_fc1,
    b_fc1,
    w_fc2,
    b_fc2,
):
    micro_count = patches.shape[0]
    outputs = []
    input_grads = []
    cond_parts = []
    summed_w = None
    summed_b = None
    ada_terms = None
    for micro_index in range(micro_count):
        cond_rows = conditioning[micro_index]
        silu_value, silu_back = jax.vjp(jax.nn.silu, cond_rows)
        silu_low = silu_value.astype(jnp.bfloat16)
        weights = gather_weights(w_qkv, w_proj, w_fc1, w_fc2, b_qv, b_proj, b_fc1, b_fc2)
        modulation = modulation_sharded(silu_low, w_ada, b_ada)
        output, saved = micro_forward(
            patches[micro_index],
            modulation,
            frame_of_slot[micro_index],
            clip_of_slot[micro_index],
            weights,
        )
        input_grad, d_modulation, grads_w, grads_b = micro_backward(
            saved, cotangent[micro_index], weights
        )
        outputs.append(output)
        input_grads.append(input_grad)
        grad_w_ada, grad_b_ada, cond_grad = ada_grads_sharded(
            silu_low, cond_rows, d_modulation, w_ada
        )
        cond_parts.append(cond_grad[None])
        ada_terms = add_terms(ada_terms, (grad_w_ada, grad_b_ada))
        part_w, part_b = reduce_grads(grads_w, grads_b)
        summed_w = add_terms(summed_w, part_w)
        summed_b = add_terms(summed_b, part_b)
    cond_all = jnp.concatenate(cond_parts, axis=0)
    return (
        jnp.stack(outputs),
        jnp.stack(input_grads),
        cond_all,
        ada_terms[0],
        ada_terms[1],
        summed_w[0],
        summed_b[0],
        summed_w[1],
        summed_b[1],
        summed_w[2],
        summed_b[2],
        summed_w[3],
        summed_b[3],
    )


def solution(mesh):
    in_specs = (
        P(None, ("dp", "fsdp"), None),
        P(None, ("dp", "fsdp"), None),
        P(),
        P(None, ("dp", "fsdp")),
        P(None, ("dp", "fsdp")),
        P("dp", "fsdp"),
        P("fsdp"),
        P("dp", "fsdp"),
        P("fsdp"),
        P("dp", "fsdp"),
        P("fsdp"),
        P("dp", "fsdp"),
        P("fsdp"),
        P("dp", "fsdp"),
        P("fsdp"),
    )
    out_specs = (
        P(None, ("dp", "fsdp"), None),
        P(None, ("dp", "fsdp"), None),
        P(None, None, "fsdp"),
        P("dp", "fsdp"),
        P("fsdp"),
        P("dp", "fsdp"),
        P("fsdp"),
        P("dp", "fsdp"),
        P("fsdp"),
        P("dp", "fsdp"),
        P("fsdp"),
        P("dp", "fsdp"),
        P("fsdp"),
    )
    return jax.shard_map(
        per_device, mesh=mesh, in_specs=in_specs, out_specs=out_specs, check_vma=False
    )
```

profile of v0, /device:TPU:0, one launch (start us, length us, event | category | flops | bytes accessed | tf_op | source)
XLA Modules:
  0.0 1921.0 jit_solution(4469489425580298956)
XLA Ops:
  14.6 38.8 %all-gather = bf16[4,864,144]{1,2,0:T(8,128)(2,1)S(1)} all-gather(bf16[1,864,144]{1,2,0:T(8,128)(2,1)S(1)} %bitcast.245), channel_id=1, replica_groups=mesh['dp'=8,'fsdp'=4] {'fsdp'}, dimensions={0}, use_global_device_ids=true | all-gather | bytes 1244160 | tf_op jit(solution)/shard_map/all_gather | solution.py:57
  55.6 15.8 all-gather.1
  73.3 24.5 %all-gather.18.cloned.1.call-done = bf16[576,1152]{0,1:T(8,128)(2,1)} async-done(((bf16[576,288]{0,1:T(8,128)(2,1)}), bf16[576,1152]{0,1:T(8,128)(2,1)}) %all-gather.18.cloned.1.call-update) | async-done | bytes 1327120 | tf_op jit(solution)/shard_map/all_gather | solution.py:60
  102.9 16.8 all-reduce.16
  119.7 13.1 all-gather.2
  135.2 69.7 %all-reduce.25.cloned.1.call-done = (f32[8,6912]{1,0:T(8,128)}, f32[8,6912]{1,0:T(8,128)}) async-done(((f32[8,6912]{1,0:T(8,128)}, f32[8,6912]{1,0:T(8,128)}), (f32[8,6912]{1,0:T(8,128)}, f32[8,6912]{1,0:T(8,128)})) %all-reduce.25.cloned.1.call-update) | async-done | bytes 442384 | tf_op jit(solution)/shard_map/psum | solution.py:141
  217.8 6.2 fusion
  238.5 12.5 all-gather.16.cloned.1.call-done
  251.0 7.1 convolution_add_fusion.1
  258.2 58.6 %all-gather.20.cloned.1.call-done = bf16[4608,1152]{1,0:T(8,128)(2,1)} async-done(((bf16[576,1152]{1,0:T(8,128)(2,1)}), bf16[4608,1152]{1,0:T(8,128)(2,1)}) %all-gather.20.cloned.1.call-update) | async-done | bytes 10616848 | tf_op jit(solution)/shard_map/all_gather | solution.py:70
  316.8 8.8 fusion.139
  331.1 8.6 fusion.141
  363.6 6.0 fusion.160
  369.7 7.6 fusion.55
  378.1 20.2 %all-reduce.15 = (bf16[1152]{0:T(1024)(128)(2,1)S(1)}, bf16[2304]{0:T(1024)(128)(2,1)}, bf16[2304]{0:T(1024)(128)(2,1)}, bf16[1152]{0:T(1024)(128)(2,1)}, bf16[1...) all-reduce(bf16[1152]{0:T(1024)(128)(2,1)S(1)} %copy-done.101, ...), channel_id=1, replica_groups=mesh['dp'=8,'fsdp'=4] {'fsdp'}, use_global_device_ids=true, to_apply=%add.2 | all-reduce | flops 19584 | bytes 78336
  399.2 6.5 convolution_add_fusion.7
  437.4 5.6 convolution_convert_fusion
  456.2 14.8 copy.162
  477.7 15.3 copy.160
  493.1 315.4 %all-reduce.23.cloned.1.call-done = (f32[8,6912]{1,0:T(8,128)}, f32[8,6912]{1,0:T(8,128)}) async-done(((f32[8,6912]{1,0:T(8,128)}, f32[8,6912]{1,0:T(8,128)}), (f32[8,6912]{1,0:T(8,128)}, f32[8,6912]{1,0:T(8,128)})) %all-reduce.23.cloned.1.call-update) | async-done | bytes 442384 | tf_op jit(solution)/shard_map/psum | solution.py:148
  825.8 168.8 %reduce-scatter.47.cloned.1.call-done = bf16[4608,288]{0,1:T(8,128)(2,1)} async-done(((bf16[4608,1152]{0,1:T(8,128)(2,1)}), bf16[4608,288]{0,1:T(8,128)(2,1)}) %reduce-scatter.47.cloned.1.call-update) | async-done | bytes 2654224 | tf_op jit(solution)/shard_map/reduce_scatter | solution.py:95
  999.5 179.6 %reduce-scatter.45.cloned.1.call-done = bf16[4608,288]{0,1:T(8,128)(2,1)} async-done(((bf16[4608,1152]{0,1:T(8,128)(2,1)}), bf16[4608,288]{0,1:T(8,128)(2,1)}) %reduce-scatter.45.cloned.1.call-update) | async-done | bytes 2654224 | tf_op jit(solution)/shard_map/reduce_scatter | solution.py:95
  1183.8 179.3 %reduce-scatter.59.cloned.1.call-done = bf16[1152,1152]{1,0:T(8,128)(2,1)} async-done(((bf16[4608,1152]{1,0:T(8,128)(2,1)}), bf16[1152,1152]{1,0:T(8,128)(2,1)}) %reduce-scatter.59.cloned.1.call-update) | async-done | bytes 2654224
  1368.5 178.4 %reduce-scatter.57.cloned.1.call-done = bf16[1152,1152]{1,0:T(8,128)(2,1)} async-done(((bf16[4608,1152]{1,0:T(8,128)(2,1)}), bf16[1152,1152]{1,0:T(8,128)(2,1)}) %reduce-scatter.57.cloned.1.call-update) | async-done | bytes 2654224
  1557.3 24.7 %all-reduce.14 = (f32[576]{0:T(1024)}, f32[288]{0:T(512)}, f32[1152]{0:T(1024)}, f32[288]{0:T(512)}) all-reduce(f32[576]{0:T(1024)S(1)} %convert_add_fusion.7, f32[288]{0:T(512)S(1)} %convert_add_fusion.9, f32[1152]{0:T(1024)S(1)} %convert_add_fusion.6, f32[288]{0:T(512)S(1)} %convert_add_fusion.8), channel_id=1, replica_groups=mesh['dp'=8,'fsdp'=4] {'dp'}, use_global_device_ids=true, to_apply=%region_36.37 | all-reduce | flops 2304 | bytes 18432 | tf_op jit(solution)/shard_map/psum | solution.py:125
  1590.9 33.9 %reduce-scatter.53.cloned.1.call-done = bf16[144,288]{1,0:T(8,128)(2,1)} async-done(((bf16[1152,288]{1,0:T(8,128)(2,1)}), bf16[144,288]{1,0:T(8,128)(2,1)}) %reduce-scatter.53.cloned.1.call-update) | async-done | bytes 82960
  1626.6 42.2 %reduce-scatter.51.cloned.1.call-done = bf16[144,864]{1,0:T(8,128)(2,1)} async-done(((bf16[1152,864]{1,0:T(8,128)(2,1)}), bf16[144,864]{1,0:T(8,128)(2,1)}) %reduce-scatter.51.cloned.1.call-update) | async-done | bytes 248848
  1669.9 43.3 %reduce-scatter.49.cloned.1.call-done = bf16[144,864]{1,0:T(8,128)(2,1)} async-done(((bf16[1152,864]{1,0:T(8,128)(2,1)}), bf16[144,864]{1,0:T(8,128)(2,1)}) %reduce-scatter.49.cloned.1.call-update) | async-done | bytes 248848
  1715.6 49.3 %reduce-scatter.63.cloned.1.call-done = bf16[576,288]{1,0:T(8,128)(2,1)} async-done(((bf16[4608,288]{1,0:T(8,128)(2,1)}), bf16[576,288]{1,0:T(8,128)(2,1)}) %reduce-scatter.63.cloned.1.call-update) | async-done | bytes 331792
  1766.1 50.2 %reduce-scatter.61.cloned.1.call-done = bf16[576,288]{1,0:T(8,128)(2,1)} async-done(((bf16[4608,288]{1,0:T(8,128)(2,1)}), bf16[576,288]{1,0:T(8,128)(2,1)}) %reduce-scatter.61.cloned.1.call-update) | async-done | bytes 331792
  1818.5 45.1 %reduce-scatter.43.cloned.1.call-done = bf16[144,1152]{1,0:T(8,128)(2,1)} async-done(((bf16[1152,1152]{1,0:T(8,128)(2,1)}), bf16[144,1152]{1,0:T(8,128)(2,1)}) %reduce-scatter.43.cloned.1.call-update) | async-done | bytes 331792 | tf_op jit(solution)/shard_map/reduce_scatter | solution.py:118
  1863.5 47.7 %reduce-scatter.41.cloned.1.call-done = bf16[144,1152]{1,0:T(8,128)(2,1)} async-done(((bf16[1152,1152]{1,0:T(8,128)(2,1)}), bf16[144,1152]{1,0:T(8,128)(2,1)}) %reduce-scatter.41.cloned.1.call-update) | async-done | bytes 331792 | tf_op jit(solution)/shard_map/reduce_scatter | solution.py:118
  (539 shorter events, 184.6 us)
Async XLA Ops:
  8.0 64.7 %all-gather.14.cloned.1.call-start = ((), (), s32[]{:S(2)}) async-start(), calls=%async_computation.18 | async-start | bytes 1658880 | tf_op jit(solution)/shard_map/all_gather | solution.py:59
  8.8 89.0 %all-gather.18.cloned.1.call-start = ((), (), s32[]{:S(2)}) async-start(), calls=%async_computation.20 | async-start | bytes 1843200 | tf_op jit(solution)/shard_map/all_gather | solution.py:60
  9.5 195.4 %all-reduce.25.cloned.1.call-start = ((), (), s32[]{:S(2)}) async-start(), calls=%async_computation.40 | async-start | bytes 884736 | tf_op jit(solution)/shard_map/psum | solution.py:141
  14.6 195.0 %all-gather.10.cloned.1.call-start = ((), (), s32[]{:S(2)}) async-start(), calls=%async_computation.16 | async-start | bytes 8957952 | tf_op jit(solution)/shard_map/all_gather | solution.py:67
  55.6 172.4 %all-gather.12.cloned.1.call-start = ((), (), s32[]{:S(2)}) async-start(), calls=%async_computation.17 | async-start | bytes 2985984 | tf_op jit(solution)/shard_map/all_gather | solution.py:68
  72.6 178.4 %all-gather.16.cloned.1.call-start = ((), (), s32[]{:S(2)}) async-start(), calls=%async_computation.19 | async-start | bytes 11943936 | tf_op jit(solution)/shard_map/all_gather | solution.py:69
  73.3 60.7 %copy-start.17 = (bf16[2,64,1152]{2,1,0:T(8,128)(2,1)S(1)}, bf16[2,64,1152]{2,1,0:T(8,128)(2,1)}, u32[]{:S(2)}) copy-start(bf16[2,64,1152]{2,1,0:T(8,128)(2,1)} %param.15) | copy-start | bytes 884740
  73.3 243.5 %all-gather.20.cloned.1.call-start = ((), (), s32[]{:S(2)}) async-start(), calls=%async_computation.21 | async-start | bytes 11943936 | tf_op jit(solution)/shard_map/all_gather | solution.py:70
  100.4 708.0 %all-reduce.23.cloned.1.call-start = ((), (), s32[]{:S(2)}) async-start(), calls=%async_computation.39 | async-start | bytes 884736 | tf_op jit(solution)/shard_map/psum | solution.py:148
  134.1 75.1 %copy-start.106 = (f32[64]{0:T(128)}, f32[64]{0:T(128)S(1)}, u32[]{:S(2)}) copy-start(f32[64]{0:T(128)S(1)} %broadcast_multiply_fusion.3) | copy-start | bytes 772
  134.1 75.1 %copy-start.109 = (f32[64]{0:T(128)}, f32[64]{0:T(128)S(1)}, u32[]{:S(2)}) copy-start(f32[64]{0:T(128)S(1)} %broadcast_multiply_fusion.1) | copy-start | bytes 772
  134.9 74.3 %copy-start.129 = (f32[64]{0:T(128)}, f32[64]{0:T(128)S(1)}, u32[]{:S(2)}) copy-start(f32[64]{0:T(128)S(1)} %fusion.129) | copy-start | bytes 772
  135.0 74.3 %copy-start.131 = (f32[64]{0:T(128)}, f32[64]{0:T(128)S(1)}, u32[]{:S(2)}) copy-start(f32[64]{0:T(128)S(1)} %fusion.131) | copy-start | bytes 772
  135.0 72.7 %copy-start.118 = (s32[64]{0:T(128)}, s32[64]{0:T(128)S(1)}, u32[]{:S(2)}) copy-start(s32[64]{0:T(128)S(1)} %get-tuple-element.151) | copy-start | bytes 772
  135.0 72.7 %copy-start.120 = (s32[64]{0:T(128)}, s32[64]{0:T(128)S(1)}, u32[]{:S(2)}) copy-start(s32[64]{0:T(128)S(1)} %get-tuple-element.152) | copy-start | bytes 772
  417.3 395.2 %reduce-scatter.39.cloned.1.call-start = ((), (), s32[]{:S(2)}) async-start(), calls=%async_computation.25 | async-start | bytes 3317760 | tf_op jit(solution)/shard_map/reduce_scatter | solution.py:89
  420.1 394.8 %reduce-scatter.37.cloned.1.call-start = ((), (), s32[]{:S(2)}) async-start(), calls=%async_computation.24 | async-start | bytes 3317760 | tf_op jit(solution)/shard_map/reduce_scatter | solution.py:89
  423.5 393.9 %reduce-scatter.35.cloned.1.call-start = ((), (), s32[]{:S(2)}) async-start(), calls=%async_computation.23 | async-start | bytes 9953280 | tf_op jit(solution)/shard_map/reduce_scatter | solution.py:86
  430.1 391.6 %reduce-scatter.33.cloned.1.call-start = ((), (), s32[]{:S(2)}) async-start(), calls=%async_computation.22 | async-start | bytes 9953280 | tf_op jit(solution)/shard_map/reduce_scatter | solution.py:86
  436.5 558.1 %reduce-scatter.47.cloned.1.call-start = ((), (), s32[]{:S(2)}) async-start(), calls=%async_computation.29 | async-start | bytes 13271040 | tf_op jit(solution)/shard_map/reduce_scatter | solution.py:95
  443.1 735.9 %reduce-scatter.45.cloned.1.call-start = ((), (), s32[]{:S(2)}) async-start(), calls=%async_computation.28 | async-start | bytes 13271040 | tf_op jit(solution)/shard_map/reduce_scatter | solution.py:95
  449.6 913.6 %reduce-scatter.59.cloned.1.call-start = ((), (), s32[]{:S(2)}) async-start(), calls=%async_computation.35 | async-start | bytes 13271040
  471.0 1075.9 %reduce-scatter.57.cloned.1.call-start = ((), (), s32[]{:S(2)}) async-start(), calls=%async_computation.34 | async-start | bytes 13271040
  493.0 1094.6 %all-reduce.21.cloned.1.call-start = ((), (), s32[]{:S(2)}) async-start(), calls=%async_computation.38 | async-start | bytes 147456 | tf_op jit(solution)/shard_map/psum | solution.py:157
  812.5 777.4 %reduce-scatter.55.cloned.1.call-start = ((), (), s32[]{:S(2)}) async-start(), calls=%async_computation.33 | async-start | bytes 995328
  814.9 809.8 %reduce-scatter.53.cloned.1.call-start = ((), (), s32[]{:S(2)}) async-start(), calls=%async_computation.32 | async-start | bytes 995328
  817.4 851.4 %reduce-scatter.51.cloned.1.call-start = ((), (), s32[]{:S(2)}) async-start(), calls=%async_computation.31 | async-start | bytes 2322432
  821.6 891.6 %reduce-scatter.49.cloned.1.call-start = ((), (), s32[]{:S(2)}) async-start(), calls=%async_computation.30 | async-start | bytes 2322432
  825.8 939.0 %reduce-scatter.63.cloned.1.call-start = ((), (), s32[]{:S(2)}) async-start(), calls=%async_computation.37 | async-start | bytes 3981312
  999.4 816.9 %reduce-scatter.61.cloned.1.call-start = ((), (), s32[]{:S(2)}) async-start(), calls=%async_computation.36 | async-start | bytes 3981312
  1183.8 679.8 %reduce-scatter.43.cloned.1.call-start = ((), (), s32[]{:S(2)}) async-start(), calls=%async_computation.27 | async-start | bytes 2985984 | tf_op jit(solution)/shard_map/reduce_scatter | solution.py:118
  1368.4 542.8 %reduce-scatter.41.cloned.1.call-start = ((), (), s32[]{:S(2)}) async-start(), calls=%async_computation.26 | async-start | bytes 2985984 | tf_op jit(solution)/shard_map/reduce_scatter | solution.py:118
  (141 other events, 917.9 us)
Sparse Core Ops, SparseCore 0:
  10.5 50.6 all-gather.13
  62.9 34.8 all-gather.17
  100.4 51.8 all-gather.9
  154.8 30.4 all-gather.11
  187.2 63.8 all-gather.15
  252.9 63.8 all-gather.19
  420.4 50.7 reduce-scatter.38
  473.6 52.8 reduce-scatter.36
  528.8 138.6 reduce-scatter.34
  669.8 140.9 reduce-scatter.32
  813.2 181.4 reduce-scatter.46
  997.0 181.9 reduce-scatter.44
  1181.4 181.7 reduce-scatter.58
  1365.5 181.3 reduce-scatter.56
  1550.0 36.2 reduce-scatter.54
  1589.7 35.0 reduce-scatter.52
  1627.9 40.8 reduce-scatter.50
  1672.4 40.8 reduce-scatter.48
  1716.7 48.0 reduce-scatter.62
  1768.2 48.0 reduce-scatter.60
  1819.8 43.7 reduce-scatter.42
  1867.4 43.7 reduce-scatter.40
Sparse Core Ops, SparseCore 1:
  16.0 188.9 all-reduce.24
  417.4 391.0 all-reduce.22
  814.5 555.3 all-reduce.20
where the time goes:
time: 1930 us; the launch traced here: 1920 us
  waiting for transfers between devices  1500 us (78%)
  matrix products  134 us (7%)
  blocking collectives  129 us (7%)
  local copies, waits for them, and re-layouts  106 us (5%)
  other arithmetic  27.3 us (1%)
  between operations  21.9 us (1%)
    unnamed x33, waiting for transfers between devices  579 us
    reduce_scatter x2, waiting for transfers between devices, reduce_grads(): lax.psum_scatter(full_w[3].astype(jnp.bfloat16), 'fsdp', scatter_dimensio...  348 us
    psum x1, waiting for transfers between devices, ada_grads_sharded(): d_total = lax.psum(d_modulation, ('dp', 'fsdp'))  315 us
    reduce_scatter x2, waiting for transfers between devices, reduce_grads(): lax.psum_scatter(inner_sums[2].astype(jnp.bfloat16), 'dp', scatter_dimens...  92.7 us
    unnamed x328, local copies, waits for them, and re-layouts  89.1 us
    psum x1, waiting for transfers between devices, modulation_sharded(): return lax.psum(padded, ('dp', 'fsdp'))  69.7 us
    all_gather x1, waiting for transfers between devices, gather_weights(): lax.all_gather(inner_parts[3], 'dp', axis=0, tiled=True)  58.6 us
    dot_general x8, matrix products, matmul_right_t(): lax.dot_general(left, right, (((1,), (1,)), ((), ())), preferred_element_...  41 us
  transfers between devices with their start and end apart: 25, of which 16 were waited for; matrix products, arithmetic and copies ran while one was open for 9% of the time, Pallas kernels for 0%

commit v1 on v0

--- a/solution.py
+++ b/solution.py
@@ -9,6 +9,27 @@
 GELU_C = math.sqrt(2.0 / math.pi)
 PRECISE = lax.Precision.HIGHEST
 NEG_FILL = -1e30
+
+
+def links_list(vec, mesh_ax):
+    n_now, finding, res = (lax.axis_size(mesh_ax), lax.axis_index(mesh_ax), vec.shape[0])
+    log = [(ix, (ix + 1) % n_now) for ix in range(n_now)]
+    queue = [(ix, (ix - 1) % n_now) for ix in range(n_now)]
+    x_now = jnp.zeros((*vec.shape[:0], n_now * res, *vec.shape[1:]), vec.dtype)
+    x_now = lax.dynamic_update_slice_in_dim(x_now, vec, finding * res, axis=0)
+    y1 = then = vec
+    oldest = n_now // 2
+    t = 1
+    while t < oldest + 1:
+        y1 = lax.ppermute(y1, mesh_ax, log)
+        x_now = lax.dynamic_update_slice_in_dim(x_now, y1, (finding - t) % n_now * res, axis=0)
+        if t < n_now - oldest:
+            then = lax.ppermute(then, axis_name=mesh_ax, perm=queue)
+            x_now = lax.dynamic_update_slice_in_dim(
+                x_now, then, (finding + t) % n_now * res, axis=0
+            )
+        t += 1
+    return x_now
 
 
 def layer_norm(values):
@@ -67,7 +88,7 @@
         lax.all_gather(inner_parts[0], "dp", axis=0, tiled=True),
         lax.all_gather(inner_parts[1], "dp", axis=0, tiled=True),
         lax.all_gather(inner_parts[2], "dp", axis=0, tiled=True),
-        lax.all_gather(inner_parts[3], "dp", axis=0, tiled=True),
+        links_list(inner_parts[3], mesh_ax="dp"),
     )
     return (
         whole_rows[0],

time: 1930 us -> 2040 us (1.057)
  local copies, waits for them, and re-layouts: 106 us -> 262 us
  waiting for transfers between devices: 1500 us -> 1450 us
    dynamic_update_slice x0 -> x8, local copies, waits for them, and re-layouts: none -> 126 us  [the longest x4 62.7 us: links_list(): lax.dynamic_update_slice_in_dim(x_now, y1, (finding - t) % n_now * res, a...]
    ppermute x0 -> x7, waiting for transfers between devices: none -> 84.1 us  [the longest x4 54.5 us: links_list(): y1 = lax.ppermute(y1, mesh_ax, log)]
    psum x1, waiting for transfers between devices: 69.7 us -> 8.89 us  [modulation_sharded(): return lax.psum(padded, ('dp', 'fsdp'))]
    all_gather x1 -> x0, waiting for transfers between devices: 58.6 us -> none  [gather_weights(): lax.all_gather(inner_parts[3], 'dp', axis=0, tiled=True)]
    unnamed x328 -> x296, local copies, waits for them, and re-layouts: 89.1 us -> 87.5 us
    unnamed x33 -> x32, waiting for transfers between devices: 579 us -> 578 us
  transfers between devices with their start and end apart: 25 -> 31, of which waited for: 16 -> 18; matrix products, arithmetic and copies ran while one was open for 9% -> 16% of each run, Pallas kernels for 0% -> 0%
where the time goes in v1:
time: 2040 us; the launch traced here: 2030 us
  waiting for transfers between devices  1450 us (71%)
  local copies, waits for them, and re-layouts  262 us (13%)
  matrix products  129 us (6%)
  blocking collectives  129 us (6%)
  other arithmetic  25.7 us (1%)
  between operations  21.9 us (1%)
    unnamed x32, waiting for transfers between devices  578 us
    reduce_scatter x2, waiting for transfers between devices, reduce_grads(): lax.psum_scatter(full_w[3].astype(jnp.bfloat16), 'fsdp', scatter_dimensio...  346 us
    psum x1, waiting for transfers between devices, ada_grads_sharded(): d_total = lax.psum(d_modulation, ('dp', 'fsdp'))  318 us
    reduce_scatter x2, waiting for transfers between devices, reduce_grads(): lax.psum_scatter(inner_sums[2].astype(jnp.bfloat16), 'dp', scatter_dimens...  92.6 us
    unnamed x296, local copies, waits for them, and re-layouts  87.5 us
    dynamic_update_slice x4, local copies, waits for them, and re-layouts, links_list(): lax.dynamic_update_slice_in_dim(x_now, y1, (finding - t) % n_now * res, a...  62.7 us
    ppermute x4, waiting for transfers between devices, links_list(): y1 = lax.ppermute(y1, mesh_ax, log)  54.5 us
    dynamic_update_slice x3, local copies, waits for them, and re-layouts, links_list(): lax.dynamic_update_slice_in_dim(x_now, then, (finding + t) % n_now * res,...  48.1 us
  transfers between devices with their start and end apart: 31, of which 18 were waited for; matrix products, arithmetic and copies ran while one was open for 16% of the time, Pallas kernels for 0%

profile of v1, /device:TPU:0, one launch (start us, length us, event | category | flops | bytes accessed | tf_op | source)
XLA Modules:
  0.0 2026.7 jit_solution(14908972775018451626)
XLA Ops:
  14.7 38.8 %all-gather = bf16[4,864,144]{1,2,0:T(8,128)(2,1)S(1)} all-gather(bf16[1,864,144]{1,2,0:T(8,128)(2,1)S(1)} %bitcast.249), channel_id=1, replica_groups=mesh['dp'=8,'fsdp'=4] {'fsdp'}, dimensions={0}, use_global_device_ids=true | all-gather | bytes 1244160 | tf_op jit(solution)/shard_map/all_gather | solution.py:78
  55.6 16.0 all-gather.1
  73.5 24.3 %all-gather.17.cloned.1.call-done = bf16[576,1152]{0,1:T(8,128)(2,1)} async-done(((bf16[576,288]{0,1:T(8,128)(2,1)}), bf16[576,1152]{0,1:T(8,128)(2,1)}) %all-gather.17.cloned.1.call-update) | async-done | bytes 1327120 | tf_op jit(solution)/shard_map/all_gather | solution.py:81
  103.0 40.4 %collective-permute-done = bf16[576,1152]{1,0:T(8,128)(2,1)} collective-permute-done((bf16[576,1152]{1,0:T(8,128)(2,1)}, bf16[576,1152]{1,0:T(8,128)(2,1)}, u32[]{:S(2)}, u32[]{:S(2)}) %collective-permute-start) | collective-permute-done | bytes 1327136 | tf_op jit(solution)/shard_map/ppermute | solution.py:24
  145.9 13.1 all-gather.2
  159.0 15.5 all-reduce.16
  181.2 29.6 %collective-permute-done.3 = bf16[576,1152]{1,0:T(8,128)(2,1)} collective-permute-done((bf16[576,1152]{1,0:T(8,128)(2,1)S(1)}, bf16[576,1152]{1,0:T(8,128)(2,1)}, u32[]{:S(2)}, u32[]{:S(2)}) %collective-permute-start.3) | collective-permute-done | bytes 1327136 | tf_op jit(solution)/shard_map/ppermute | solution.py:27
  213.8 9.4 collective-permute-done.4
  242.6 14.8 dynamic_update_slice.45
  260.1 16.1 dynamic_update_slice.46
  278.8 16.7 dynamic_update_slice.47
  298.2 14.7 dynamic_update_slice.48
  315.5 14.8 dynamic_update_slice.49
  332.9 16.6 dynamic_update_slice.50
  352.1 16.6 dynamic_update_slice.51
  371.4 15.3 dynamic_update_slice.52
  474.0 21.0 %all-reduce.15 = (bf16[1152]{0:T(1024)(128)(2,1)S(1)}, bf16[2304]{0:T(1024)(128)(2,1)S(1)}, bf16[2304]{0:T(1024)(128)(2,1)}, bf16[1152]{0:T(1024)(128)(2,1)}, bf...) all-reduce(bf16[1152]{0:T(1024)(128)(2,1)S(1)} %copy-done.100, ...), channel_id=1, replica_groups=mesh['dp'=8,'fsdp'=4] {'fsdp'}, use_global_device_ids=true, to_apply=%add.2 | all-reduce | flops 19584 | bytes 78336
  561.2 15.3 copy.170
  583.3 15.1 copy.168
  598.4 317.8 %all-reduce.23.cloned.1.call-done = (f32[8,6912]{1,0:T(8,128)}, f32[8,6912]{1,0:T(8,128)}) async-done(((f32[8,6912]{1,0:T(8,128)}, f32[8,6912]{1,0:T(8,128)}), (f32[8,6912]{1,0:T(8,128)}, f32[8,6912]{1,0:T(8,128)})) %all-reduce.23.cloned.1.call-update) | async-done | bytes 442384 | tf_op jit(solution)/shard_map/psum | solution.py:169
  934.0 166.4 %reduce-scatter.47.cloned.1.call-done = bf16[4608,288]{0,1:T(8,128)(2,1)} async-done(((bf16[4608,1152]{0,1:T(8,128)(2,1)}), bf16[4608,288]{0,1:T(8,128)(2,1)}) %reduce-scatter.47.cloned.1.call-update) | async-done | bytes 2654224 | tf_op jit(solution)/shard_map/reduce_scatter | solution.py:116
  1105.2 179.7 %reduce-scatter.45.cloned.1.call-done = bf16[4608,288]{0,1:T(8,128)(2,1)} async-done(((bf16[4608,1152]{0,1:T(8,128)(2,1)}), bf16[4608,288]{0,1:T(8,128)(2,1)}) %reduce-scatter.45.cloned.1.call-update) | async-done | bytes 2654224 | tf_op jit(solution)/shard_map/reduce_scatter | solution.py:116
  1289.6 179.3 %reduce-scatter.59.cloned.1.call-done = bf16[1152,1152]{1,0:T(8,128)(2,1)} async-done(((bf16[4608,1152]{1,0:T(8,128)(2,1)}), bf16[1152,1152]{1,0:T(8,128)(2,1)}) %reduce-scatter.59.cloned.1.call-update) | async-done | bytes 2654224
  1474.2 178.6 %reduce-scatter.57.cloned.1.call-done = bf16[1152,1152]{1,0:T(8,128)(2,1)} async-done(((bf16[4608,1152]{1,0:T(8,128)(2,1)}), bf16[1152,1152]{1,0:T(8,128)(2,1)}) %reduce-scatter.57.cloned.1.call-update) | async-done | bytes 2654224
  1663.2 24.7 %all-reduce.14 = (f32[576]{0:T(1024)}, f32[288]{0:T(512)}, f32[1152]{0:T(1024)}, f32[288]{0:T(512)}) all-reduce(f32[576]{0:T(1024)S(1)} %convert_add_fusion.7, f32[288]{0:T(512)S(1)} %convert_add_fusion.9, f32[1152]{0:T(1024)S(1)} %convert_add_fusion.6, f32[288]{0:T(512)S(1)} %convert_add_fusion.8), channel_id=1, replica_groups=mesh['dp'=8,'fsdp'=4] {'dp'}, use_global_device_ids=true, to_apply=%region_36.37 | all-reduce | flops 2304 | bytes 18432 | tf_op jit(solution)/shard_map/psum | solution.py:146
  1697.4 33.3 %reduce-scatter.53.cloned.1.call-done = bf16[144,288]{1,0:T(8,128)(2,1)} async-done(((bf16[1152,288]{1,0:T(8,128)(2,1)}), bf16[144,288]{1,0:T(8,128)(2,1)}) %reduce-scatter.53.cloned.1.call-update) | async-done | bytes 82960
  1732.6 42.2 %reduce-scatter.51.cloned.1.call-done = bf16[144,864]{1,0:T(8,128)(2,1)} async-done(((bf16[1152,864]{1,0:T(8,128)(2,1)}), bf16[144,864]{1,0:T(8,128)(2,1)}) %reduce-scatter.51.cloned.1.call-update) | async-done | bytes 248848
  1775.9 43.3 %reduce-scatter.49.cloned.1.call-done = bf16[144,864]{1,0:T(8,128)(2,1)} async-done(((bf16[1152,864]{1,0:T(8,128)(2,1)}), bf16[144,864]{1,0:T(8,128)(2,1)}) %reduce-scatter.49.cloned.1.call-update) | async-done | bytes 248848
  1821.5 49.1 %reduce-scatter.63.cloned.1.call-done = bf16[576,288]{1,0:T(8,128)(2,1)} async-done(((bf16[4608,288]{1,0:T(8,128)(2,1)}), bf16[576,288]{1,0:T(8,128)(2,1)}) %reduce-scatter.63.cloned.1.call-update) | async-done | bytes 331792
  1871.8 50.4 %reduce-scatter.61.cloned.1.call-done = bf16[576,288]{1,0:T(8,128)(2,1)} async-done(((bf16[4608,288]{1,0:T(8,128)(2,1)}), bf16[576,288]{1,0:T(8,128)(2,1)}) %reduce-scatter.61.cloned.1.call-update) | async-done | bytes 331792
  1924.4 44.9 %reduce-scatter.43.cloned.1.call-done = bf16[144,1152]{1,0:T(8,128)(2,1)} async-done(((bf16[1152,1152]{1,0:T(8,128)(2,1)}), bf16[144,1152]{1,0:T(8,128)(2,1)}) %reduce-scatter.43.cloned.1.call-update) | async-done | bytes 331792 | tf_op jit(solution)/shard_map/reduce_scatter | solution.py:139
  1969.3 47.7 %reduce-scatter.41.cloned.1.call-done = bf16[144,1152]{1,0:T(8,128)(2,1)} async-done(((bf16[1152,1152]{1,0:T(8,128)(2,1)}), bf16[144,1152]{1,0:T(8,128)(2,1)}) %reduce-scatter.41.cloned.1.call-update) | async-done | bytes 331792 | tf_op jit(solution)/shard_map/reduce_scatter | solution.py:139
  (536 shorter events, 283.5 us)
Async XLA Ops:
  8.0 64.9 %all-gather.13.cloned.1.call-start = ((), (), s32[]{:S(2)}) async-start(), calls=%async_computation.18 | async-start | bytes 1658880 | tf_op jit(solution)/shard_map/all_gather | solution.py:80
  8.8 89.0 %all-gather.17.cloned.1.call-start = ((), (), s32[]{:S(2)}) async-start(), calls=%async_computation.20 | async-start | bytes 1843200 | tf_op jit(solution)/shard_map/all_gather | solution.py:81
  9.5 223.9 %all-reduce.25.cloned.1.call-start = ((), (), s32[]{:S(2)}) async-start(), calls=%async_computation.39 | async-start | bytes 884736 | tf_op jit(solution)/shard_map/psum | solution.py:162
  14.6 372.1 %all-gather.9.cloned.1.call-start = ((), (), s32[]{:S(2)}) async-start(), calls=%async_computation.16 | async-start | bytes 8957952 | tf_op jit(solution)/shard_map/all_gather | solution.py:88
  55.6 355.8 %all-gather.11.cloned.1.call-start = ((), (), s32[]{:S(2)}) async-start(), calls=%async_computation.17 | async-start | bytes 2985984 | tf_op jit(solution)/shard_map/all_gather | solution.py:89
  72.8 346.3 %all-gather.15.cloned.1.call-start = ((), (), s32[]{:S(2)}) async-start(), calls=%async_computation.19 | async-start | bytes 11943936 | tf_op jit(solution)/shard_map/all_gather | solution.py:90
  73.5 842.8 %all-reduce.23.cloned.1.call-start = ((), (), s32[]{:S(2)}) async-start(), calls=%async_computation.38 | async-start | bytes 884736 | tf_op jit(solution)/shard_map/psum | solution.py:169
  100.4 43.0 %collective-permute-start = (bf16[576,1152]{1,0:T(8,128)(2,1)}, bf16[576,1152]{1,0:T(8,128)(2,1)}, u32[]{:S(2)}, u32[]{:S(2)}) collective-permute-start(bf16[576,1152]{1,0:T(8,128)(2,1)} %copy.122), channel_id=1, source_target_pairs={{0,4},{4,8},{8,12},{12,16},{16,20},{20,24},{24,28},{28,0},{1,5},{5... | collective-permute-start | bytes 3981320 | tf_op jit(solution)/shard_map/ppermute | solution.py:24
  100.4 74.7 %collective-permute-start.1 = (bf16[576,1152]{1,0:T(8,128)(2,1)}, bf16[576,1152]{1,0:T(8,128)(2,1)S(1)}, u32[]{:S(2)}, u32[]{:S(2)}) collective-permute-start(bf16[576,1152]{1,0:T(8,128)(2,1)} %copy.122), channel_id=1, source_target_pairs={{0,28},{4,0},{8,4},{12,8},{16,12},{20,16},{24,20},{28,24},{1,29},{... | collective-permute-start | bytes 3981320 | tf_op jit(solution)/shard_map/ppermute | solution.py:27
  143.4 36.4 %collective-permute-start.2 = (bf16[576,1152]{1,0:T(8,128)(2,1)}, bf16[576,1152]{1,0:T(8,128)(2,1)}, u32[]{:S(2)}, u32[]{:S(2)}) collective-permute-start(bf16[576,1152]{1,0:T(8,128)(2,1)} %collective-permute-done), channel_id=1, source_target_pairs={{0,4},{4,8},{8,12},{12,16},{16,20},{20,24},{24,28},{28,0},{1,5},{5... | collective-permute-start | bytes 3981320 | tf_op jit(solution)/shard_map/ppermute | solution.py:24
  175.1 35.8 %collective-permute-start.3 = (bf16[576,1152]{1,0:T(8,128)(2,1)S(1)}, bf16[576,1152]{1,0:T(8,128)(2,1)}, u32[]{:S(2)}, u32[]{:S(2)}) collective-permute-start(bf16[576,1152]{1,0:T(8,128)(2,1)S(1)} %collective-permute-done.1), channel_id=1, source_target_pairs={{0,28},{4,0},{8,4},{12,8},{16,12},{20,16},{24,20},{28,24},{1,29},{... | collective-permute-start | bytes 3981320 | tf_op jit(solution)/shard_map/ppermute | solution.py:27
  179.8 43.4 %collective-permute-start.4 = (bf16[576,1152]{1,0:T(8,128)(2,1)}, bf16[576,1152]{1,0:T(8,128)(2,1)}, u32[]{:S(2)}, u32[]{:S(2)}) collective-permute-start(bf16[576,1152]{1,0:T(8,128)(2,1)} %collective-permute-done.2), channel_id=1, source_target_pairs={{0,4},{4,8},{8,12},{12,16},{16,20},{20,24},{24,28},{28,0},{1,5},{5... | collective-permute-start | bytes 3981320 | tf_op jit(solution)/shard_map/ppermute | solution.py:24
  210.8 138.7 %collective-permute-start.5 = (bf16[576,1152]{1,0:T(8,128)(2,1)}, bf16[576,1152]{1,0:T(8,128)(2,1)}, u32[]{:S(2)}, u32[]{:S(2)}) collective-permute-start(bf16[576,1152]{1,0:T(8,128)(2,1)} %collective-permute-done.3), channel_id=1, source_target_pairs={{0,28},{4,0},{8,4},{12,8},{16,12},{20,16},{24,20},{28,24},{1,29},{... | collective-permute-start | bytes 3981320 | tf_op jit(solution)/shard_map/ppermute | solution.py:27
  223.2 145.6 %collective-permute-start.6 = (bf16[576,1152]{1,0:T(8,128)(2,1)}, bf16[576,1152]{1,0:T(8,128)(2,1)}, u32[]{:S(2)}, u32[]{:S(2)}) collective-permute-start(bf16[576,1152]{1,0:T(8,128)(2,1)} %collective-permute-done.4), channel_id=1, source_target_pairs={{0,4},{4,8},{8,12},{12,16},{16,20},{20,24},{24,28},{28,0},{1,5},{5... | collective-permute-start | bytes 3981320 | tf_op jit(solution)/shard_map/ppermute | solution.py:24
  235.3 197.0 %copy-start.3 = (f32[64,6912]{1,0:T(8,128)}, f32[64,6912]{1,0:T(8,128)S(1)}, u32[]{:S(2)}) copy-start(f32[64,6912]{1,0:T(8,128)S(1)} %fusion.108) | copy-start | bytes 5308420
  522.4 397.9 %reduce-scatter.39.cloned.1.call-start = ((), (), s32[]{:S(2)}) async-start(), calls=%async_computation.24 | async-start | bytes 3317760 | tf_op jit(solution)/shard_map/reduce_scatter | solution.py:110
  525.1 397.9 %reduce-scatter.37.cloned.1.call-start = ((), (), s32[]{:S(2)}) async-start(), calls=%async_computation.23 | async-start | bytes 3317760 | tf_op jit(solution)/shard_map/reduce_scatter | solution.py:110
  528.5 397.0 %reduce-scatter.35.cloned.1.call-start = ((), (), s32[]{:S(2)}) async-start(), calls=%async_computation.22 | async-start | bytes 9953280 | tf_op jit(solution)/shard_map/reduce_scatter | solution.py:107
  534.9 394.8 %reduce-scatter.33.cloned.1.call-start = ((), (), s32[]{:S(2)}) async-start(), calls=%async_computation.21 | async-start | bytes 9953280 | tf_op jit(solution)/shard_map/reduce_scatter | solution.py:107
  541.4 559.0 %reduce-scatter.47.cloned.1.call-start = ((), (), s32[]{:S(2)}) async-start(), calls=%async_computation.28 | async-start | bytes 13271040 | tf_op jit(solution)/shard_map/reduce_scatter | solution.py:116
  548.0 736.9 %reduce-scatter.45.cloned.1.call-start = ((), (), s32[]{:S(2)}) async-start(), calls=%async_computation.27 | async-start | bytes 13271040 | tf_op jit(solution)/shard_map/reduce_scatter | solution.py:116
  554.4 914.5 %reduce-scatter.59.cloned.1.call-start = ((), (), s32[]{:S(2)}) async-start(), calls=%async_computation.34 | async-start | bytes 13271040
  576.5 1076.3 %reduce-scatter.57.cloned.1.call-start = ((), (), s32[]{:S(2)}) async-start(), calls=%async_computation.33 | async-start | bytes 13271040
  598.4 1095.8 %all-reduce.21.cloned.1.call-start = ((), (), s32[]{:S(2)}) async-start(), calls=%async_computation.37 | async-start | bytes 147456 | tf_op jit(solution)/shard_map/psum | solution.py:178
  920.3 776.1 %reduce-scatter.55.cloned.1.call-start = ((), (), s32[]{:S(2)}) async-start(), calls=%async_computation.32 | async-start | bytes 995328
  922.8 807.9 %reduce-scatter.53.cloned.1.call-start = ((), (), s32[]{:S(2)}) async-start(), calls=%async_computation.31 | async-start | bytes 995328
  925.4 849.4 %reduce-scatter.51.cloned.1.call-start = ((), (), s32[]{:S(2)}) async-start(), calls=%async_computation.30 | async-start | bytes 2322432
  929.7 889.4 %reduce-scatter.49.cloned.1.call-start = ((), (), s32[]{:S(2)}) async-start(), calls=%async_computation.29 | async-start | bytes 2322432
  933.9 936.7 %reduce-scatter.63.cloned.1.call-start = ((), (), s32[]{:S(2)}) async-start(), calls=%async_computation.36 | async-start | bytes 3981312
  1105.1 817.1 %reduce-scatter.61.cloned.1.call-start = ((), (), s32[]{:S(2)}) async-start(), calls=%async_computation.35 | async-start | bytes 3981312
  1289.6 679.7 %reduce-scatter.43.cloned.1.call-start = ((), (), s32[]{:S(2)}) async-start(), calls=%async_computation.26 | async-start | bytes 2985984 | tf_op jit(solution)/shard_map/reduce_scatter | solution.py:139
  1474.1 542.8 %reduce-scatter.41.cloned.1.call-start = ((), (), s32[]{:S(2)}) async-start(), calls=%async_computation.25 | async-start | bytes 2985984 | tf_op jit(solution)/shard_map/reduce_scatter | solution.py:139
  (131 other events, 2297.5 us)
Sparse Core Ops, SparseCore 0:
  10.5 50.6 all-gather.12
  62.8 34.9 all-gather.16
  100.4 73.5 all-gather.8
  176.5 40.2 all-gather.10
  218.7 78.3 all-gather.14
  525.3 51.8 reduce-scatter.38
  579.5 52.7 reduce-scatter.36
  634.6 138.6 reduce-scatter.34
  775.8 140.8 reduce-scatter.32
  918.9 181.4 reduce-scatter.46
  1102.8 181.9 reduce-scatter.44
  1287.1 181.7 reduce-scatter.58
  1471.3 181.3 reduce-scatter.56
  1655.9 36.2 reduce-scatter.54
  1695.6 35.0 reduce-scatter.52
  1733.9 40.7 reduce-scatter.50
  1778.3 40.7 reduce-scatter.48
  1822.5 48.0 reduce-scatter.62
  1874.1 48.0 reduce-scatter.60
  1925.5 43.7 reduce-scatter.42
  1973.2 43.7 reduce-scatter.40
Sparse Core Ops, SparseCore 1:
  16.0 217.4 all-reduce.24
  522.5 393.7 all-reduce.22
  922.4 553.2 all-reduce.20
